TPU v7x, 128 devices: a whole 4x4x4 slice. The times are simulated.
128 devices in a mesh: pts: 4 (over x_lo, core), comp: 32 (over x_hi, y, z).
Axes of the slice: x: 4 (x_hi: 2, x_lo: 2; x = x_hi * 2 + x_lo), y: 4, z: 4, core: 2. Of those that a mesh axis runs over, the one named last changes fastest.
Arguments:
- points: bfloat16 [1536, 512], P(('pts', 'comp')), may hold values from -28 to 28
- centres: bfloat16 [2048, 512], P('comp'), may hold values from -5 to 5
- whitening: bfloat16 [2048, 512, 512], P('comp', 'pts'), as said below
- log_prior: float32 [2048], P('comp'), may hold values from -4 to 4
Outputs:
- counts: float32 [2048], P('comp')
- first_moments: float32 [2048, 512], P('comp')
- second_moments: float32 [2048, 512, 512], P('comp', 'pts')
Inputs may be any that keep to these rules, and one draw needn't show every extreme that they name: Each whitening[k] is lower triangular with diagonal entries between 0.69 and 2.82.
All inputs are finite; a program needn't handle non-finite values.
Results may differ from a plain program's by a relative error of at most 0.0029.
Values may be sent and summed in bfloat16 or wider, within the bound.
No kernel may reach another device: no remote copies, remote signals or barrier semaphores. Data moves between devices by JAX's collectives and lax.ppermute only.
A program may use at most 128 MiB of HBM per device.

v0:
```python
import jax
import jax.numpy as jnp
from jax import lax
from jax.sharding import PartitionSpec as P

D = 512
anneal_beta = 1.25


def normalise(partial_total, prior_col):
    logits = anneal_beta * (prior_col - partial_total / D)
    row_peak = lax.pmax(jnp.max(logits, axis=0), "comp")
    expo_vals = jnp.exp(logits - row_peak[None, :])
    row_total = lax.psum(jnp.sum(expo_vals, axis=0), "comp")
    return (expo_vals / row_total[None, :]).astype(jnp.bfloat16)


def body(points, centres, whitening, log_prior):
    gathered = lax.all_gather(points, ("pts", "comp"), axis=0, tiled=True)
    comp_here = whitening.shape[0]
    band_rows = whitening.shape[1]
    total_points = gathered.shape[0]
    band_start = lax.axis_index("pts") * band_rows
    block_count = comp_here // 8
    factor_blocks = whitening.reshape(block_count, 8, band_rows, D)
    centre_blocks = centres.reshape(block_count, 8, D)

    def block_term(pair):
        factor, centre = pair
        offset = jnp.einsum("kqd,kd->kq", factor, centre, preferred_element_type=jnp.float32)
        whitened = (
            jnp.einsum("kqd,nd->kqn", factor, gathered, preferred_element_type=jnp.float32)
            - offset[:, :, None]
        )
        square_cols = lax.dynamic_slice_in_dim(factor, band_start, band_rows, 2)
        diag_vals = jnp.diagonal(square_cols, axis1=1, axis2=2).astype(jnp.float32)
        return (
            0.5 * jnp.sum(whitened * whitened, axis=1)
            - jnp.sum(jnp.log(diag_vals), axis=1)[:, None]
        )

    partial_term = lax.map(block_term, (factor_blocks, centre_blocks)).reshape(
        comp_here, total_points
    )
    prior_col = log_prior[:, None]
    summed = lax.psum(partial_term, "pts")
    responsibility = normalise(summed, prior_col)
    counts = jnp.sum(responsibility.astype(jnp.float32), axis=1)
    first_moments = jnp.dot(responsibility, gathered, preferred_element_type=jnp.float32)
    band_points = lax.dynamic_slice_in_dim(gathered, band_start, band_rows, 1).T.astype(jnp.float32)

    def block_second(resp_block):
        weighted = (resp_block.astype(jnp.float32)[:, None, :] * band_points[None, :, :]).astype(
            jnp.bfloat16
        )
        return jnp.einsum("kqn,nd->kqd", weighted, gathered, preferred_element_type=jnp.float32)

    second_moments = lax.map(block_second, responsibility.reshape(block_count, 8, total_points))
    return (counts, first_moments, second_moments.reshape(comp_here, band_rows, D))


def solution(mesh):
    in_specs = (P(("pts", "comp"), None), P("comp", None), P("comp", "pts", None), P("comp"))
    out_specs = (P("comp"), P("comp", None), P("comp", "pts", None))
    return jax.shard_map(body, mesh=mesh, in_specs=in_specs, out_specs=out_specs, check_vma=False)
```

profile of v0, /device:TPU:0, one launch (start us, length us, event | category | flops | bytes accessed | tf_op | source)
XLA Modules:
  0.0 677.8 jit_solution(2913701126033206041)
XLA Ops:
  8.0 305.8 %all-gather.3.cloned.1.call-done = bf16[128,12,512]{2,1,0:T(8,128)(2,1)} async-done(((bf16[1,12,512]{2,1,0:T(8,128)(2,1)}), bf16[128,12,512]{2,1,0:T(8,128)(2,1)}) %all-gather.3.cloned.1.call-update) | async-done | bytes 1572880 | tf_op jit(solution)/shard_map/all_gather | solution.py:19
  313.8 2.5 reshape.85
  316.3 99.1 %while.23 = (s32[]{:T(128)}, f32[8,8,1536]{2,1,0:T(8,128)}, bf16[8,8,128,512]{3,2,1,0:T(8,128)(2,1)}, bf16[1536,512]{1,0:T(8,128)(2,1)S(1)}, bf16[8,8,512]{2,1,0...) while((s32[]{:T(128)}, f32[8,8,1536]{2,1,0:T(8,128)}, bf16[8,8,128,512]{3,2,1,0:T(8,128)(2,1)}, ...), condition=%wide.region_3.4_spmd, body=%wide.region_0.3_spmd.sunk | while | flops 1616394752 | bytes 4908217 | solution.py:42
  316.3 0.7 dynamic-slice_bitcast_fusion.2
  317.0 1.6 fusion.30
  318.6 3.1 multiply_reduce_fusion.2
  321.7 1.2 constant_dynamic-slice_fusion.2
  322.9 3.1 copy.20
  325.9 2.0 gather_fusion
  328.7 0.7 dynamic-slice_bitcast_fusion.2
  329.4 1.6 fusion.30
  331.0 3.1 multiply_reduce_fusion.2
  334.1 1.2 constant_dynamic-slice_fusion.2
  335.3 3.1 copy.20
  338.3 2.0 gather_fusion
  341.1 0.7 dynamic-slice_bitcast_fusion.2
  341.8 1.6 fusion.30
  343.3 3.1 multiply_reduce_fusion.2
  346.4 1.2 constant_dynamic-slice_fusion.2
  347.6 3.1 copy.20
  350.7 2.0 gather_fusion
  354.1 1.6 fusion.30
  355.7 3.1 multiply_reduce_fusion.2
  358.8 1.2 constant_dynamic-slice_fusion.2
  360.0 3.1 copy.20
  363.1 2.0 gather_fusion
  366.5 1.6 fusion.30
  368.1 3.1 multiply_reduce_fusion.2
  371.2 1.2 constant_dynamic-slice_fusion.2
  372.4 3.1 copy.20
  375.5 2.0 gather_fusion
  378.2 0.7 dynamic-slice_bitcast_fusion.2
  378.9 1.6 fusion.30
  380.5 3.1 multiply_reduce_fusion.2
  383.6 1.2 constant_dynamic-slice_fusion.2
  384.8 3.1 copy.20
  387.9 2.0 gather_fusion
  390.6 0.7 dynamic-slice_bitcast_fusion.2
  391.3 1.6 fusion.30
  392.9 3.1 multiply_reduce_fusion.2
  396.0 1.2 constant_dynamic-slice_fusion.2
  397.2 3.1 copy.20
  400.2 2.0 gather_fusion
  403.7 1.6 fusion.30
  405.3 3.1 multiply_reduce_fusion.2
  408.3 1.2 constant_dynamic-slice_fusion.2
  409.5 3.1 copy.20
  412.6 2.0 gather_fusion
  415.7 38.1 %all-reduce.2.cloned.1.call-done = f32[64,1536]{1,0:T(8,128)} async-done(((f32[64,1536]{1,0:T(8,128)}), f32[64,1536]{1,0:T(8,128)}) %all-reduce.2.cloned.1.call-update) | async-done | bytes 393232 | tf_op jit(solution)/shard_map/psum | solution.py:46
  453.9 1.1 fusion.15
  455.0 97.2 %pmax.7 = f32[1536]{0:T(1024)S(1)} all-reduce(f32[1536]{0:T(1024)S(1)} %fusion.15), channel_id=1, replica_groups=mesh['pts'=4,'comp'=32] {'comp'}, use_global_device_ids=true, to_apply=%region_6.7 | all-reduce | flops 1536 | bytes 12288 | tf_op jit(solution)/shard_map/pmax | solution.py:12
  552.2 1.2 fusion.14
  553.3 90.0 %psum.15 = f32[1536]{0:T(1024)S(1)} all-reduce(f32[1536]{0:T(1024)S(1)} %fusion.14), channel_id=1, replica_groups=mesh['pts'=4,'comp'=32] {'comp'}, use_global_device_ids=true, to_apply=%region_8.9 | all-reduce | flops 1536 | bytes 12288 | tf_op jit(solution)/shard_map/psum | solution.py:14
  643.3 1.8 convert_reduce_fusion
  645.1 1.0 fusion.16
  646.1 24.9 %while.24 = (s32[]{:T(128)}, f32[8,8,128,512]{3,2,1,0:T(8,128)}, bf16[8,8,1536]{2,1,0:T(8,128)(2,1)S(1)}, f32[128,1536]{1,0:T(8,128)S(1)}, bf16[1536,512]{1,0:T(8,128)(2,1)S(1)}, /*index=5*/s32[]{:T(128)}) while((s32[]{:T(128)}, f32[8,8,128,512]{3,2,1,0:T(8,128)}, bf16[8,8,1536]{2,1,0:T(8,128)(2,1)S(1)}, f32[128,1536]{1,0:T(8,128)S(1)}, ...), condition=%wide.region_11.12_spmd, body=%wide.region_10.11_spmd.sunk | while | flops 1613770752 | bytes 4579913 | solution.py:58
  646.1 3.1 bitcast_dynamic-update-slice_fusion.2
  649.2 3.1 bitcast_dynamic-update-slice_fusion.2
  652.4 3.1 bitcast_dynamic-update-slice_fusion.2
  655.5 3.1 bitcast_dynamic-update-slice_fusion.2
  658.6 3.1 bitcast_dynamic-update-slice_fusion.2
  661.7 3.1 bitcast_dynamic-update-slice_fusion.2
  664.8 3.1 bitcast_dynamic-update-slice_fusion.2
  667.9 3.1 bitcast_dynamic-update-slice_fusion.2
  (45 shorter events, 9.1 us)
Async XLA Ops:
  7.2 306.6 %all-gather.3.cloned.1.call-start = ((), (), s32[]{:S(2)}) async-start(), calls=%async_computation.1 | async-start | bytes 2113536 | tf_op jit(solution)/shard_map/all_gather | solution.py:19
  7.9 446.0 %all-reduce.2.cloned.1.call-start = ((), (), s32[]{:S(2)}) async-start(), calls=%async_computation | async-start | bytes 786432 | tf_op jit(solution)/shard_map/psum | solution.py:46
  316.3 137.6 %copy-start = (f32[64]{0:T(128)S(1)}, f32[64]{0:T(128)}, u32[]{:S(2)}) copy-start(f32[64]{0:T(128)} %param.11) | copy-start | bytes 772
Sparse Core Ops, SparseCore 0:
  9.7 304.0 all-gather.2
  415.5 38.3 all-reduce.1
where the time goes:
time: 680 us; the launch traced here: 678 us
  waiting for transfers between devices  345 us (51%)
  blocking collectives  187 us (28%)
  matrix products  63.2 us (9%)
  local copies, waits for them, and re-layouts  58.3 us (9%)
  between operations  14.1 us (2%)
  other arithmetic  10.1 us (1%)
    all_gather x1, waiting for transfers between devices, body(): gathered = lax.all_gather(points, ('pts', 'comp'), axis=0, tiled=True)  306 us
    pmax x1, blocking collectives, normalise(): row_peak = lax.pmax(jnp.max(logits, axis=0), 'comp')  97.2 us
    psum x1, blocking collectives, normalise(): row_total = lax.psum(jnp.sum(expo_vals, axis=0), 'comp')  90 us
    psum x1, waiting for transfers between devices, body(): summed = lax.psum(partial_term, 'pts')  38.1 us
    dynamic_slice x16, local copies, waits for them, and re-layouts, block_term(): square_cols = lax.dynamic_slice_in_dim(factor, band_start, band_rows, 2)  34.1 us
    dot_general x8, matrix products, block_second(): jnp.einsum('kqn,nd->kqd', weighted, gathered, preferred_element_type=jnp....  24.8 us
    dot_general x8, matrix products, block_term(): jnp.einsum('kqd,nd->kqn', factor, gathered, preferred_element_type=jnp.fl...  24.7 us
    gather x8, local copies, waits for them, and re-layouts, block_term(): diag_vals = jnp.diagonal(square_cols, axis1=1, axis2=2).astype(jnp.float32)  15.9 us
  transfers between devices with their start and end apart: 2, of which 2 were waited for; matrix products, arithmetic and copies ran while one was open for 0% of the time, Pallas kernels for 0%

commit v1 on v0

--- a/solution.py
+++ b/solution.py
@@ -5,6 +5,13 @@
 
 D = 512
 anneal_beta = 1.25
+
+
+def exchange_gather(value, name, along):
+    peers = lax.axis_size(name)
+    shards = jnp.stack([value for _ in range(peers)])
+    shards = lax.all_to_all(shards, name, split_axis=0, concat_axis=0)
+    return jnp.concatenate(shards, axis=along)
 
 
 def normalise(partial_total, prior_col):
@@ -16,7 +23,7 @@
 
 
 def body(points, centres, whitening, log_prior):
-    gathered = lax.all_gather(points, ("pts", "comp"), axis=0, tiled=True)
+    gathered = exchange_gather(points, ("pts", "comp"), 0)
     comp_here = whitening.shape[0]
     band_rows = whitening.shape[1]
     total_points = gathered.shape[0]

time: 680 us -> 415 us (0.61)
  waiting for transfers between devices: 345 us -> 61.6 us
  starting transfers between devices: 0.08 us -> 11.2 us
    all_gather x1 -> x0, waiting for transfers between devices: 306 us -> none  [body(): gathered = lax.all_gather(points, ('pts', 'comp'), axis=0, tiled=True)]
    all_to_all x0 -> x1, waiting for transfers between devices: none -> 28.7 us  [exchange_gather(): shards = lax.all_to_all(shards, name, split_axis=0, concat_axis=0)]
    all_to_all x0 -> x1, starting transfers between devices: none -> 11.2 us  [exchange_gather(): shards = lax.all_to_all(shards, name, split_axis=0, concat_axis=0)]
where the time goes in v1:
time: 415 us; the launch traced here: 414 us
  blocking collectives  187 us (45%)
  matrix products  68.7 us (17%)
  waiting for transfers between devices  61.6 us (15%)
  local copies, waits for them, and re-layouts  59.5 us (14%)
  between operations  14.1 us (3%)
  starting transfers between devices  11.2 us (3%)
  other arithmetic  11.2 us (3%)
    pmax x1, blocking collectives, normalise(): row_peak = lax.pmax(jnp.max(logits, axis=0), 'comp')  97.2 us
    psum x1, blocking collectives, normalise(): row_total = lax.psum(jnp.sum(expo_vals, axis=0), 'comp')  90 us
    dynamic_slice x16, local copies, waits for them, and re-layouts, block_term(): square_cols = lax.dynamic_slice_in_dim(factor, band_start, band_rows, 2)  34.1 us
    psum x1, waiting for transfers between devices, body(): summed = lax.psum(partial_term, 'pts')  32.8 us
    all_to_all x1, waiting for transfers between devices, exchange_gather(): shards = lax.all_to_all(shards, name, split_axis=0, concat_axis=0)  28.7 us
    dot_general x8, matrix products, block_term(): jnp.einsum('kqd,nd->kqn', factor, gathered, preferred_element_type=jnp.fl...  28.7 us
    dot_general x8, matrix products, block_second(): jnp.einsum('kqn,nd->kqd', weighted, gathered, preferred_element_type=jnp....  24.8 us
    gather x8, local copies, waits for them, and re-layouts, block_term(): diag_vals = jnp.diagonal(square_cols, axis1=1, axis2=2).astype(jnp.float32)  15.9 us
  transfers between devices with their start and end apart: 2, of which 2 were waited for; matrix products, arithmetic and copies ran while one was open for 0% of the time, Pallas kernels for 0%

profile of v1, /device:TPU:0, one launch (start us, length us, event | category | flops | bytes accessed | tf_op | source)
XLA Modules:
  0.0 413.6 jit_solution(5923604404470989325)
XLA Ops:
  7.2 2.3 stack.2
  9.5 11.2 %all-to-all-start = ((bf16[128,12,512]{2,1,0:T(8,128)(2,1)}), bf16[128,12,512]{2,1,0:T(8,128)(2,1)S(1)}, u32[]{:S(2)}, u32[]{:S(2)}) async-start(bf16[128,12,512]{2,1,0:T(8,128)(2,1)} %stack.2), calls=%async_computation | async-start | bytes 4194304 | tf_op jit(solution)/shard_map/all_to_all | solution.py:13
  20.7 28.7 %all-to-all-done = bf16[128,12,512]{2,1,0:T(8,128)(2,1)S(1)} async-done(((bf16[128,12,512]{2,1,0:T(8,128)(2,1)}), bf16[128,12,512]{2,1,0:T(8,128)(2,1)S(1)}, u32[]{:S(2)}, u32[]{:S(2)}) %all-to-all-start) | async-done | bytes 1572896 | tf_op jit(solution)/shard_map/all_to_all | solution.py:13
  49.4 1.3 reshape.78
  50.8 103.1 %while.23 = (s32[]{:T(128)}, f32[8,8,1536]{2,1,0:T(8,128)}, bf16[8,8,128,512]{3,2,1,0:T(8,128)(2,1)}, bf16[1536,512]{1,0:T(8,128)(2,1)}, bf16[8,8,512]{2,1,0:T(8...) while((s32[]{:T(128)}, f32[8,8,1536]{2,1,0:T(8,128)}, bf16[8,8,128,512]{3,2,1,0:T(8,128)(2,1)}, ...), condition=%wide.region_3.4_spmd, body=%wide.region_0.3_spmd.sunk | while | flops 1616394752 | bytes 4908217 | solution.py:49
  50.8 0.7 dynamic-slice_bitcast_fusion.2
  51.5 1.6 fusion.30
  53.1 3.6 multiply_reduce_fusion.2
  56.7 1.2 constant_dynamic-slice_fusion.2
  57.9 3.1 copy.18
  61.0 2.0 gather_fusion
  63.7 0.7 dynamic-slice_bitcast_fusion.2
  64.4 1.6 fusion.30
  66.0 3.6 multiply_reduce_fusion.2
  69.6 1.2 constant_dynamic-slice_fusion.2
  70.8 3.1 copy.18
  73.8 2.0 gather_fusion
  77.3 1.6 fusion.30
  78.8 3.6 multiply_reduce_fusion.2
  82.4 1.2 constant_dynamic-slice_fusion.2
  83.6 3.1 copy.18
  86.7 2.0 gather_fusion
  90.1 1.6 fusion.30
  91.7 3.6 multiply_reduce_fusion.2
  95.3 1.2 constant_dynamic-slice_fusion.2
  96.5 3.1 copy.18
  99.6 2.0 gather_fusion
  103.0 1.6 fusion.30
  104.6 3.6 multiply_reduce_fusion.2
  108.2 1.2 constant_dynamic-slice_fusion.2
  109.4 3.1 copy.18
  112.5 2.0 gather_fusion
  115.9 1.6 fusion.30
  117.5 3.6 multiply_reduce_fusion.2
  121.1 1.2 constant_dynamic-slice_fusion.2
  122.3 3.1 copy.18
  125.4 2.0 gather_fusion
  128.8 1.6 fusion.30
  130.4 3.6 multiply_reduce_fusion.2
  134.0 1.2 constant_dynamic-slice_fusion.2
  135.2 3.1 copy.18
  138.3 2.0 gather_fusion
  141.7 1.6 fusion.30
  143.3 3.6 multiply_reduce_fusion.2
  146.9 1.2 constant_dynamic-slice_fusion.2
  148.1 3.1 copy.18
  151.2 2.0 gather_fusion
  153.9 1.2 convert_bitcast_fusion
  155.4 32.8 %all-reduce.2.cloned.1.call-done = f32[64,1536]{1,0:T(8,128)} async-done(((f32[64,1536]{1,0:T(8,128)}), f32[64,1536]{1,0:T(8,128)}) %all-reduce.2.cloned.1.call-update) | async-done | bytes 393232 | tf_op jit(solution)/shard_map/psum | solution.py:53
  188.2 1.1 fusion.15
  189.3 97.2 %pmax.7 = f32[1536]{0:T(1024)S(1)} all-reduce(f32[1536]{0:T(1024)S(1)} %fusion.15), channel_id=1, replica_groups=mesh['pts'=4,'comp'=32] {'comp'}, use_global_device_ids=true, to_apply=%region_6.7 | all-reduce | flops 1536 | bytes 12288 | tf_op jit(solution)/shard_map/pmax | solution.py:19
  286.5 1.2 fusion.14
  287.7 90.0 %psum.15 = f32[1536]{0:T(1024)S(1)} all-reduce(f32[1536]{0:T(1024)S(1)} %fusion.14), channel_id=1, replica_groups=mesh['pts'=4,'comp'=32] {'comp'}, use_global_device_ids=true, to_apply=%region_8.9 | all-reduce | flops 1536 | bytes 12288 | tf_op jit(solution)/shard_map/psum | solution.py:21
  377.6 1.8 convert_reduce_fusion
  379.4 2.4 fusion.16
  381.9 24.9 %while.24 = (s32[]{:T(128)}, f32[8,8,128,512]{3,2,1,0:T(8,128)}, bf16[8,8,1536]{2,1,0:T(8,128)(2,1)S(1)}, f32[128,1536]{1,0:T(8,128)S(1)}, bf16[1536,512]{1,0:T(8,128)(2,1)S(1)}, /*index=5*/s32[]{:T(128)}) while((s32[]{:T(128)}, f32[8,8,128,512]{3,2,1,0:T(8,128)}, bf16[8,8,1536]{2,1,0:T(8,128)(2,1)S(1)}, f32[128,1536]{1,0:T(8,128)S(1)}, ...), condition=%wide.region_11.12_spmd, body=%wide.region_10.11_spmd.sunk | while | flops 1613770752 | bytes 4579913 | solution.py:65
  381.9 3.1 bitcast_dynamic-update-slice_fusion.2
  385.0 3.1 bitcast_dynamic-update-slice_fusion.2
  388.1 3.1 bitcast_dynamic-update-slice_fusion.2
  391.2 3.1 bitcast_dynamic-update-slice_fusion.2
  394.3 3.1 bitcast_dynamic-update-slice_fusion.2
  397.4 3.1 bitcast_dynamic-update-slice_fusion.2
  400.5 3.1 bitcast_dynamic-update-slice_fusion.2
  403.6 3.1 bitcast_dynamic-update-slice_fusion.2
  (47 shorter events, 10.5 us)
Async XLA Ops:
  9.5 40.0 %all-to-all-start = ((bf16[128,12,512]{2,1,0:T(8,128)(2,1)}), bf16[128,12,512]{2,1,0:T(8,128)(2,1)S(1)}, u32[]{:S(2)}, u32[]{:S(2)}) async-start(bf16[128,12,512]{2,1,0:T(8,128)(2,1)} %stack.2), calls=%async_computation | async-start | bytes 4194304 | tf_op jit(solution)/shard_map/all_to_all | solution.py:13
  20.6 167.5 %all-reduce.2.cloned.1.call-start = ((), (), s32[]{:S(2)}) async-start(), calls=%async_computation.1 | async-start | bytes 786432 | tf_op jit(solution)/shard_map/psum | solution.py:53
  50.8 137.4 %copy-start.1 = (f32[64]{0:T(128)S(1)}, f32[64]{0:T(128)}, u32[]{:S(2)}) copy-start(f32[64]{0:T(128)} %param.11) | copy-start | bytes 772
  153.9 228.0 %copy-start = (bf16[1536,512]{1,0:T(8,128)(2,1)S(1)}, bf16[1536,512]{1,0:T(8,128)(2,1)}, u32[]{:S(2)}) copy-start(bf16[1536,512]{1,0:T(8,128)(2,1)} %get-tuple-element.294) | copy-start | bytes 4718596
Sparse Core Ops, SparseCore 0:
  154.0 34.1 all-reduce.1
